TPU v7x, 32 devices: a whole 2x2x4 slice. The times are simulated.
32 devices in a mesh: dp: 2 (over x), tensor: 4 (over z), fsdp: 4 (over y, core).
Axes of the slice: x: 2, y: 2, z: 4, core: 2. Of those that a mesh axis runs over, the one named last changes fastest.
Arguments:
- train_acts: bfloat16 [2048, 4096], P(('dp', 'fsdp'), 'tensor'), may hold values from -6 to 6
- val_acts: bfloat16 [2048, 4096], P(('dp', 'fsdp'), 'tensor'), may hold values from -6 to 6
- train_cot: bfloat16 [2048, 4096], P(('dp', 'fsdp'), 'tensor'), may hold values from -6 to 6
- val_cot: bfloat16 [2048, 4096], P(('dp', 'fsdp'), 'tensor'), may hold values from -6 to 6
- train_lengths: int32 [32], P(('dp', 'fsdp')), may hold values from 16 to 64
- val_lengths: int32 [32], P(('dp', 'fsdp')), may hold values from 16 to 64
- gate_weight: bfloat16 [4096, 11008], P(('dp', 'fsdp'), 'tensor'), may hold values from -0.09375 to 0.09375
- up_weight: bfloat16 [4096, 11008], P(('dp', 'fsdp'), 'tensor'), may hold values from -0.09375 to 0.09375
- in_basis: bfloat16 [11008, 64], P('tensor'), may hold values from -0.0546875 to 0.0546875
- out_basis: bfloat16 [4096, 128], P('tensor'), may hold values from -0.09375 to 0.09375
Outputs:
- scores: float32 [32, 32], P(('dp', 'fsdp'))
Inputs may be any that keep to these rules, and one draw needn't show every extreme that they name: `train_lengths`: an example's first length slots hold its tokens, the rest are padding. `val_lengths`: as for the training examples.
All inputs are finite; a program needn't handle non-finite values.
Results may differ from a plain program's by a relative error of at most 0.004.
Values may be sent and summed in bfloat16 or wider, within the bound.
No kernel may reach another device: no remote copies, remote signals or barrier semaphores. Data moves between devices by JAX's collectives and lax.ppermute only.
A program may use at most 128 MiB of HBM per device.

v0:
```python
import jax
import jax.numpy as jnp
from jax import lax
from jax.sharding import PartitionSpec as P

SEQ = 64


def outer_sums(in_proj, out_proj, valid):
    in_three = in_proj.reshape(valid.shape[0], valid.shape[1], in_proj.shape[1]) * valid[:, :, None]
    out_three = out_proj.reshape(valid.shape[0], valid.shape[1], out_proj.shape[1])
    return jnp.einsum("esj,esk->ejk", in_three, out_three, precision=lax.Precision.HIGHEST)


def on_device(
    train_acts,
    val_acts,
    train_cot,
    val_cot,
    train_lengths,
    val_lengths,
    gate_weight,
    up_weight,
    in_basis,
    out_basis,
):
    train_full, val_full = (
        lax.all_gather(train_acts, "tensor", axis=1, tiled=True),
        lax.all_gather(val_acts, "tensor", axis=1, tiled=True),
    )
    activations = jnp.concatenate([train_full, val_full], axis=0)
    cotangents = jnp.concatenate([train_cot, val_cot], axis=0)
    gate_sum = jnp.dot(
        activations,
        lax.all_gather(gate_weight, ("dp", "fsdp"), axis=0, tiled=True),
        preferred_element_type=jnp.float32,
    )
    up_sum = jnp.dot(
        activations,
        lax.all_gather(up_weight, ("dp", "fsdp"), axis=0, tiled=True),
        preferred_element_type=jnp.float32,
    )
    hidden = (jax.nn.silu(gate_sum) * up_sum).astype(jnp.bfloat16)
    in_part = jnp.dot(hidden, in_basis, preferred_element_type=jnp.float32)
    out_part = jnp.dot(cotangents, out_basis, preferred_element_type=jnp.float32)
    lengths = jnp.concatenate([train_lengths, val_lengths], axis=0)
    valid = (jnp.arange(SEQ, dtype=jnp.int32)[None, :] < lengths[:, None]).astype(jnp.float32)
    in_proj, out_proj = lax.psum((in_part, out_part), "tensor")
    sketch = outer_sums(in_proj, out_proj, valid)
    flat_sketch = sketch.reshape(sketch.shape[0], sketch.shape[1] * sketch.shape[2])
    unit_rows = flat_sketch * lax.rsqrt(
        jnp.sum(flat_sketch * flat_sketch, axis=1, keepdims=True) + 1e-06
    )
    train_count = train_lengths.shape[0]
    train_unit = unit_rows[:train_count]
    val_local = unit_rows[train_count:]
    width_all = flat_sketch.shape[1]
    share = width_all // lax.axis_size("tensor")
    first = lax.axis_index("tensor") * share
    train_share = lax.dynamic_slice_in_dim(train_unit, first, share, 1)
    val_share_local = lax.dynamic_slice_in_dim(val_local, first, share, 1)
    val_share = lax.all_gather(val_share_local, ("dp", "fsdp"), axis=0, tiled=True)
    partial_scores = jnp.dot(
        train_share,
        val_share.T,
        precision=lax.Precision.HIGHEST,
        preferred_element_type=jnp.float32,
    )
    product = lax.psum(partial_scores, "tensor")
    return product * jnp.sqrt(jnp.float32(width_all))


def solution(mesh):
    placed = (
        P(("dp", "fsdp"), "tensor"),
        P(("dp", "fsdp"), "tensor"),
        P(("dp", "fsdp"), "tensor"),
        P(("dp", "fsdp"), "tensor"),
        P(("dp", "fsdp")),
        P(("dp", "fsdp")),
        P(("dp", "fsdp"), "tensor"),
        P(("dp", "fsdp"), "tensor"),
        P("tensor", None),
        P("tensor", None),
    )
    return jax.shard_map(
        on_device, mesh=mesh, in_specs=placed, out_specs=P(("dp", "fsdp"), None), check_vma=False
    )
```

profile of v0, /device:TPU:0, one launch (start us, length us, event | category | flops | bytes accessed | tf_op | source)
XLA Modules:
  0.0 431.9 jit_solution(13203272675145067068)
XLA Ops:
  6.5 0.0 copy-start
  6.5 0.0 copy-start.2
  6.5 0.0 copy-start.1
  6.5 0.0 copy-start.3
  6.5 0.0 all-gather.6.cloned.1.call-start
  6.6 0.7 all-gather.6.cloned.1.call-update
  7.3 0.0 all-gather.8.cloned.1.call-start
  7.3 0.7 all-gather.8.cloned.1.call-update
  8.0 0.0 all-gather.10.cloned.1.call-start
  8.1 0.7 all-gather.10.cloned.1.call-update
  8.8 0.0 all-gather.12.cloned.1.call-start
  8.8 0.5 all-gather.12.cloned.1.call-update
  9.3 0.0 all-reduce.3.cloned.1.call-start
  9.4 0.0 copy-done.2
  9.4 0.0 copy-done.1
  9.4 0.0 copy-done.3
  9.4 1.1 fusion.1
  10.6 46.8 %all-gather.6.cloned.1.call-done = bf16[256,4096]{1,0:T(8,128)(2,1)} async-done(((bf16[256,1024]{1,0:T(8,128)(2,1)}), bf16[256,4096]{1,0:T(8,128)(2,1)}) %all-gather.6.cloned.1.call-update) | async-done | bytes 2097168 | tf_op jit(solution)/shard_map/all_gather | solution.py:28
  57.3 3.1 constant_dynamic-update-slice_fusion.1
  60.4 42.9 %all-gather.8.cloned.1.call-done = bf16[256,4096]{1,0:T(8,128)(2,1)} async-done(((bf16[256,1024]{1,0:T(8,128)(2,1)}), bf16[256,4096]{1,0:T(8,128)(2,1)}) %all-gather.8.cloned.1.call-update) | async-done | bytes 2097168 | tf_op jit(solution)/shard_map/all_gather | solution.py:29
  103.4 3.1 constant_dynamic-update-slice_fusion
  106.5 116.1 %all-gather.10.cloned.1.call-done = bf16[4096,2752]{0,1:T(8,128)(2,1)} async-done(((bf16[512,2752]{0,1:T(8,128)(2,1)}), bf16[4096,2752]{0,1:T(8,128)(2,1)}) %all-gather.10.cloned.1.call-update) | async-done | bytes 22544400 | tf_op jit(solution)/shard_map/all_gather | solution.py:35
  222.7 19.2 %fusion.15 = f32[512,2752]{0,1:T(8,128)} fusion(bf16[512,4096]{1,0:T(8,128)(2,1)} %constant_dynamic-update-slice_fusion, bf16[4096,2752]{0,1:T(8,128)(2,1)} %all-gather.10.cloned.1.call-done), kind=kOutput, calls=%fused_computation.25 | convolution fusion | flops 11542724608 | bytes 32374784 | tf_op jit(solution)/shard_map/dot_general | solution.py:33
  241.9 0.0 copy-start.4
  241.9 0.0 copy-start.5
  241.9 101.1 %all-gather.12.cloned.1.call-done = bf16[4096,2752]{0,1:T(8,128)(2,1)} async-done(((bf16[512,2752]{0,1:T(8,128)(2,1)}), bf16[4096,2752]{0,1:T(8,128)(2,1)}) %all-gather.12.cloned.1.call-update) | async-done | bytes 22544400 | tf_op jit(solution)/shard_map/all_gather | solution.py:40
  343.0 0.0 copy-done
  343.0 20.0 %fusion = f32[512,64]{0,1:T(8,128)S(1)} fusion(bf16[2752,64]{0,1:T(8,128)(2,1)S(1)} %copy-done, f32[512,2752]{0,1:T(8,128)} %fusion.15, bf16[512,4096]{1,0:T(8,128)(2,1)} %constant_dynamic-update-slice_fusion, bf16[4096,2752]{0,1:T(8,128)(2,1)} %all-gather.12.cloned.1.call-done), kind=kOutput, calls=%fused_computation.1 | convolution fusion | flops 11731533824 | bytes 32858112 | tf_op jit(solution)/shard_map/dot_general | solution.py:44
  363.1 0.1 reshape.37
  363.2 0.8 copy.12
  363.9 0.0 all-reduce.3.cloned.1.call-update
  363.9 0.0 copy-done.4
  364.0 0.0 copy-done.5
  364.0 0.1 pad_add_fusion
  364.0 0.1 fusion.10
  364.1 38.7 %all-reduce.3.cloned.1.call-done = (f32[8,64,128]{2,1,0:T(8,128)}, f32[8,64,64]{1,2,0:T(8,128)}) async-done(((f32[8,64,128]{2,1,0:T(8,128)}, f32[8,64,64]{1,2,0:T(8,128)}), (f32[8,64,128]{2,1,0:T(8,128)}, f32[8,64,64]{1,2,0:T(8,128)})) %all-reduce.3.cloned.1.call-update) | async-done | bytes 393232 | tf_op jit(solution)/shard_map/psum | solution.py:48
  402.8 1.5 multiply_reduce_fusion
  404.3 0.2 bitcast_multiply_fusion
  404.6 9.3 %all-gather = f32[8,4,2048]{2,1,0:T(4,128)S(1)} all-gather(f32[1,4,2048]{2,1,0:T(4,128)S(1)} %dynamic-slice_bitcast_fusion), channel_id=1, replica_groups=mesh['dp'=2,'tensor'=4,'fsdp'=4] {'dp','fsdp'}, dimensions={0}, use_global_device_ids=true | all-gather | bytes 294912 | tf_op jit(solution)/shard_map/all_gather | solution.py:62
  413.8 0.1 reshape.41
  413.9 0.3 fusion.8
  414.2 10.6 %psum.23 = f32[4,32]{1,0:T(4,128)S(1)} all-reduce(f32[4,32]{1,0:T(4,128)S(1)} %fusion.8), channel_id=1, replica_groups=mesh['dp'=2,'tensor'=4,'fsdp'=4] {'tensor'}, use_global_device_ids=true, to_apply=%region_3.4 | all-reduce | flops 128 | bytes 1024 | tf_op jit(solution)/shard_map/psum | solution.py:69
  424.8 0.6 broadcast_multiply_fusion
  (3 shorter events, 0.1 us)
Async XLA Ops:
  6.5 336.5 %copy-start = (bf16[2752,64]{0,1:T(8,128)(2,1)S(1)}, bf16[2752,64]{0,1:T(8,128)(2,1)}, u32[]{:S(2)}) copy-start(bf16[2752,64]{0,1:T(8,128)(2,1)} %param.18) | copy-start | bytes 1056772
  6.5 2.8 copy-start.2
  6.5 2.9 copy-start.1
  6.5 2.9 copy-start.3
  6.5 50.8 %all-gather.6.cloned.1.call-start = ((), (), s32[]{:S(2)}) async-start(), calls=%async_computation | async-start | bytes 2621440 | tf_op jit(solution)/shard_map/all_gather | solution.py:28
  7.3 96.1 %all-gather.8.cloned.1.call-start = ((), (), s32[]{:S(2)}) async-start(), calls=%async_computation.1 | async-start | bytes 2621440 | tf_op jit(solution)/shard_map/all_gather | solution.py:29
  8.0 214.7 %all-gather.10.cloned.1.call-start = ((), (), s32[]{:S(2)}) async-start(), calls=%async_computation.2 | async-start | bytes 25362432 | tf_op jit(solution)/shard_map/all_gather | solution.py:35
  8.8 334.3 %all-gather.12.cloned.1.call-start = ((), (), s32[]{:S(2)}) async-start(), calls=%async_computation.3 | async-start | bytes 25362432 | tf_op jit(solution)/shard_map/all_gather | solution.py:40
  9.3 393.4 %all-reduce.3.cloned.1.call-start = ((), (), s32[]{:S(2)}) async-start(), calls=%async_computation.4 | async-start | bytes 1048576 | tf_op jit(solution)/shard_map/psum | solution.py:48
  241.9 122.1 %copy-start.4 = (s32[4]{0:T(128)S(1)}, s32[4]{0:T(128)}, u32[]{:S(2)}) copy-start(s32[4]{0:T(128)} %param.15) | copy-start | bytes 52
  241.9 122.1 %copy-start.5 = (s32[4]{0:T(128)S(1)}, s32[4]{0:T(128)}, u32[]{:S(2)}) copy-start(s32[4]{0:T(128)} %param.14) | copy-start | bytes 52
Sparse Core Ops, SparseCore 0:
  8.9 48.3 all-gather.5
  58.9 44.4 all-gather.7
  105.3 117.3 all-gather.9
  224.4 118.5 all-gather.11
  364.1 38.6 all-reduce.2
where the time goes:
time: 432 us
  waiting for transfers between devices  348 us (81%)
  matrix products  42.2 us (10%)
  blocking collectives  19.9 us (5%)
  between operations  13.2 us (3%)
  local copies, waits for them, and re-layouts  7.28 us (2%)
    all_gather x1, waiting for transfers between devices, on_device(): lax.all_gather(gate_weight, ('dp', 'fsdp'), axis=0, tiled=True)  116 us
    all_gather x1, waiting for transfers between devices, on_device(): lax.all_gather(up_weight, ('dp', 'fsdp'), axis=0, tiled=True)  101 us
    all_gather x1, waiting for transfers between devices, on_device(): lax.all_gather(train_acts, 'tensor', axis=1, tiled=True)  46.8 us
    all_gather x1, waiting for transfers between devices, on_device(): lax.all_gather(val_acts, 'tensor', axis=1, tiled=True)  42.9 us
    psum x1, waiting for transfers between devices, on_device(): in_proj, out_proj = lax.psum((in_part, out_part), 'tensor')  38.7 us
    dot_general x1, matrix products, on_device(): in_part = jnp.dot(hidden, in_basis, preferred_element_type=jnp.float32)  20 us
    dot_general x1, matrix products, on_device(): jnp.dot(activations, lax.all_gather(gate_weight, ('dp', 'fsdp'), axis=0,...  19.2 us
    psum x1, blocking collectives, on_device(): product = lax.psum(partial_scores, 'tensor')  10.6 us
  transfers between devices with their start and end apart: 5, of which 5 were waited for; matrix products, arithmetic and copies ran while one was open for 6% of the time, Pallas kernels for 0%

commit v1 on v0

--- a/solution.py
+++ b/solution.py
@@ -35,11 +35,24 @@
         lax.all_gather(gate_weight, ("dp", "fsdp"), axis=0, tiled=True),
         preferred_element_type=jnp.float32,
     )
-    up_sum = jnp.dot(
-        activations,
-        lax.all_gather(up_weight, ("dp", "fsdp"), axis=0, tiled=True),
-        preferred_element_type=jnp.float32,
-    )
+
+    def register_roads(xs):
+        wide_n = lax.axis_size(("dp", "fsdp"))
+        cards = [(k0, (k0 + 1) % wide_n) for k0 in range(wide_n)]
+        column = [(k0, (k0 - 1) % wide_n) for k0 in range(wide_n)]
+        built, y = ([xs], [xs])
+        for _ in range(wide_n // 2):
+            built.append(lax.ppermute(built[-1], axis_name=("dp", "fsdp"), perm=cards))
+        for _ in tuple(range((wide_n - 1) // 2)):
+            y.append(lax.ppermute(y[-1], axis_name=("dp", "fsdp"), perm=column))
+        main = jnp.roll(
+            jnp.concatenate([*built[::-1], *y[1:]], axis=0),
+            (lax.axis_index(("dp", "fsdp")) - wide_n // 2) * xs.shape[0],
+            axis=0,
+        )
+        return main
+
+    up_sum = jnp.dot(activations, register_roads(up_weight), preferred_element_type=jnp.float32)
     hidden = (jax.nn.silu(gate_sum) * up_sum).astype(jnp.bfloat16)
     in_part = jnp.dot(hidden, in_basis, preferred_element_type=jnp.float32)
     out_part = jnp.dot(cotangents, out_basis, preferred_element_type=jnp.float32)

time: 432 us -> 474 us (1.097)
  waiting for transfers between devices: 348 us -> 210 us
  starting transfers between devices: 0.18 us -> 135 us
  local copies, waits for them, and re-layouts: 7.28 us -> 52 us
    ppermute x0 -> x7, starting transfers between devices: none -> 134 us  [the longest x4 132 us: register_roads(): built.append(lax.ppermute(built[-1], axis_name=('dp', 'fsdp'), perm=cards))]
    ppermute x0 -> x7, waiting for transfers between devices: none -> 128 us  [the longest x4 72.1 us: register_roads(): built.append(lax.ppermute(built[-1], axis_name=('dp', 'fsdp'), perm=cards))]
    all_gather x1, waiting for transfers between devices: 116 us -> 0.01 us  [on_device(): lax.all_gather(gate_weight, ('dp', 'fsdp'), axis=0, tiled=True)]
    all_gather x1 -> x0, waiting for transfers between devices: 101 us -> none  [on_device(): lax.all_gather(up_weight, ('dp', 'fsdp'), axis=0, tiled=True)]
    all_gather x1, waiting for transfers between devices: 46.8 us -> 0.01 us  [on_device(): lax.all_gather(train_acts, 'tensor', axis=1, tiled=True)]
    unnamed x15 -> x30, local copies, waits for them, and re-layouts: 3.24 us -> 46.2 us
    all_gather x1, waiting for transfers between devices: 42.9 us -> 0.01 us  [on_device(): lax.all_gather(val_acts, 'tensor', axis=1, tiled=True)]
    psum x1, waiting for transfers between devices: 38.7 us -> 80.1 us  [on_device(): in_proj, out_proj = lax.psum((in_part, out_part), 'tensor')]
  transfers between devices with their start and end apart: 5 -> 11, of which waited for: 5 -> 5; matrix products, arithmetic and copies ran while one was open for 6% -> 11% of each run, Pallas kernels for 0% -> 0%
where the time goes in v1:
time: 474 us
  waiting for transfers between devices  210 us (44%)
  starting transfers between devices  135 us (28%)
  local copies, waits for them, and re-layouts  52 us (11%)
  matrix products  43.3 us (9%)
  blocking collectives  19.9 us (4%)
  between operations  13.2 us (3%)
    ppermute x4, starting transfers between devices, register_roads(): built.append(lax.ppermute(built[-1], axis_name=('dp', 'fsdp'), perm=cards))  132 us
    psum x1, waiting for transfers between devices, on_device(): in_proj, out_proj = lax.psum((in_part, out_part), 'tensor')  80.1 us
    ppermute x4, waiting for transfers between devices, register_roads(): built.append(lax.ppermute(built[-1], axis_name=('dp', 'fsdp'), perm=cards))  72.1 us
    ppermute x3, waiting for transfers between devices, register_roads(): y.append(lax.ppermute(y[-1], axis_name=('dp', 'fsdp'), perm=column))  55.6 us
    unnamed x30, local copies, waits for them, and re-layouts  46.2 us
    dot_general x1, matrix products, on_device(): in_part = jnp.dot(hidden, in_basis, preferred_element_type=jnp.float32)  20.1 us
    dot_general x1, matrix products, on_device(): jnp.dot(activations, lax.all_gather(gate_weight, ('dp', 'fsdp'), axis=0,...  19.1 us
    psum x1, blocking collectives, on_device(): product = lax.psum(partial_scores, 'tensor')  10.6 us
  transfers between devices with their start and end apart: 11, of which 5 were waited for; matrix products, arithmetic and copies ran while one was open for 11% of the time, Pallas kernels for 0%

profile of v1, /device:TPU:0, one launch (start us, length us, event | category | flops | bytes accessed | tf_op | source)
XLA Modules:
  0.0 473.8 jit_solution(13475752835851372447)
XLA Ops:
  6.5 0.7 all-gather.5.cloned.1.call-update
  7.3 0.0 all-gather.7.cloned.1.call-start
  7.3 0.7 all-gather.7.cloned.1.call-update
  8.0 0.0 all-gather.9.cloned.1.call-start
  8.1 0.7 all-gather.9.cloned.1.call-update
  8.7 0.0 all-reduce.3.cloned.1.call-start
  8.8 0.5 collective-permute-start
  9.3 34.5 %collective-permute-done = bf16[512,2752]{0,1:T(8,128)(2,1)S(1)} collective-permute-done((bf16[512,2752]{0,1:T(8,128)(2,1)}, bf16[512,2752]{0,1:T(8,128)(2,1)S(1)}, u32[]{:S(2)}, u32[]{:S(2)}) %collective-permute-start) | collective-permute-done | bytes 2818080 | tf_op jit(solution)/shard_map/ppermute | solution.py:45
  43.9 2.6 collective-permute-start.4
  46.5 31.5 %collective-permute-done.1 = bf16[512,2752]{0,1:T(8,128)(2,1)S(1)} collective-permute-done((bf16[512,2752]{0,1:T(8,128)(2,1)S(1)}, bf16[512,2752]{0,1:T(8,128)(2,1)S(1)}, u32[]{:S(2)}, u32[]{:S(2)}) %collective-permute-start.1) | collective-permute-done | bytes 2818080 | tf_op jit(solution)/shard_map/ppermute | solution.py:45
  78.0 1.6 copy-done.2
  79.6 28.2 %collective-permute-start.2 = (bf16[512,2752]{0,1:T(8,128)(2,1)S(1)}, bf16[512,2752]{0,1:T(8,128)(2,1)}, u32[]{:S(2)}, u32[]{:S(2)}) collective-permute-start(bf16[512,2752]{0,1:T(8,128)(2,1)S(1)} %collective-permute-done.1), channel_id=1, source_target_pairs={{0,1},{1,2},{2,3},{3,16},{16,17},{17,18},{18,19},{19,0},{4,5},{5,6... | collective-permute-start | bytes 8454152 | tf_op jit(solution)/shard_map/ppermute | solution.py:45
  107.8 6.1 %collective-permute-done.2 = bf16[512,2752]{0,1:T(8,128)(2,1)} collective-permute-done((bf16[512,2752]{0,1:T(8,128)(2,1)S(1)}, bf16[512,2752]{0,1:T(8,128)(2,1)}, u32[]{:S(2)}, u32[]{:S(2)}) %collective-permute-start.2) | collective-permute-done | bytes 2818080 | tf_op jit(solution)/shard_map/ppermute | solution.py:45
  113.9 103.0 %collective-permute-start.3 = (bf16[512,2752]{0,1:T(8,128)(2,1)}, bf16[512,2752]{0,1:T(8,128)(2,1)}, u32[]{:S(2)}, u32[]{:S(2)}) collective-permute-start(bf16[512,2752]{0,1:T(8,128)(2,1)} %collective-permute-done.2), channel_id=1, source_target_pairs={{0,1},{1,2},{2,3},{3,16},{16,17},{17,18},{18,19},{19,0},{4,5},{5,6... | collective-permute-start | bytes 8454152 | tf_op jit(solution)/shard_map/ppermute | solution.py:45
  216.9 2.4 fusion.8
  219.3 3.1 constant_dynamic-update-slice_fusion.1
  222.5 3.1 constant_dynamic-update-slice_fusion
  225.6 3.7 constant_dynamic-update-slice_fusion.17
  229.3 3.6 constant_dynamic-update-slice_fusion.16
  232.9 1.8 constant_dynamic-update-slice_fusion.15
  234.7 1.8 constant_dynamic-update-slice_fusion.14
  236.4 1.8 constant_dynamic-update-slice_fusion.13
  238.2 3.6 constant_dynamic-update-slice_fusion.12
  241.8 3.6 constant_dynamic-update-slice_fusion.11
  245.4 55.6 %collective-permute-done.6 = bf16[512,2752]{0,1:T(8,128)(2,1)S(1)} collective-permute-done((bf16[512,2752]{0,1:T(8,128)(2,1)}, bf16[512,2752]{0,1:T(8,128)(2,1)S(1)}, u32[]{:S(2)}, u32[]{:S(2)}) %collective-permute-start.6) | collective-permute-done | bytes 2818080 | tf_op jit(solution)/shard_map/ppermute | solution.py:47
  301.0 1.9 constant_dynamic-update-slice_fusion.10
  302.9 3.7 constant_dynamic-update-slice_fusion.9
  306.5 3.7 constant_dynamic-update-slice_fusion.8
  310.2 1.8 constant_dynamic-update-slice_fusion.7
  312.0 1.8 constant_dynamic-update-slice_fusion.6
  313.7 1.7 constant_dynamic-update-slice_fusion.5
  315.5 3.6 constant_dynamic-update-slice_fusion.4
  319.1 3.5 constant_dynamic-update-slice_fusion.3
  322.6 1.7 constant_dynamic-update-slice_fusion.2
  324.3 19.1 %fusion.24 = f32[512,2752]{0,1:T(8,128)} fusion(bf16[512,4096]{1,0:T(8,128)(2,1)} %constant_dynamic-update-slice_fusion, bf16[4096,2752]{0,1:T(8,128)(2,1)} %all-gather.9.cloned.1.call-done), kind=kOutput, calls=%fused_computation.45 | convolution fusion | flops 11542724608 | bytes 32374784 | tf_op jit(solution)/shard_map/dot_general | solution.py:33
  343.4 20.1 %fusion.5 = f32[512,64]{0,1:T(8,128)S(1)} fusion(bf16[2752,64]{0,1:T(8,128)(2,1)S(1)} %copy-done, f32[512,2752]{0,1:T(8,128)} %fusion.24, bf16[512,4096]{1,0:T(8,128)(2,1)} %constant_dynamic-update-slice_fusion, bf16[8192,2752]{0,1:T(8,128)(2,1)} %constant_dynamic-update-slice_fusion.2, s32[]{:T(128)S(6)} %select_n.18), kind=kOutput, calls=%fused_computation.3 | convolution fusion | flops 11731533824 | bytes 32858116 | tf_op jit(solution)/shard_map/dot_general | solution.py:57
  363.5 0.1 reshape.37
  363.6 0.8 copy.12
  364.4 0.1 pad_add_fusion
  364.5 0.1 fusion.17
  364.6 80.1 %all-reduce.3.cloned.1.call-done = (f32[8,64,128]{2,1,0:T(8,128)}, f32[8,64,64]{1,2,0:T(8,128)}) async-done(((f32[8,64,128]{2,1,0:T(8,128)}, f32[8,64,64]{1,2,0:T(8,128)}), (f32[8,64,128]{2,1,0:T(8,128)}, f32[8,64,64]{1,2,0:T(8,128)})) %all-reduce.3.cloned.1.call-update) | async-done | bytes 393232 | tf_op jit(solution)/shard_map/psum | solution.py:61
  444.6 1.5 multiply_reduce_fusion
  446.2 0.2 bitcast_multiply_fusion
  446.4 9.3 %all-gather = f32[8,4,2048]{2,1,0:T(4,128)S(1)} all-gather(f32[1,4,2048]{2,1,0:T(4,128)S(1)} %dynamic-slice_bitcast_fusion), channel_id=1, replica_groups=mesh['dp'=2,'tensor'=4,'fsdp'=4] {'dp','fsdp'}, dimensions={0}, use_global_device_ids=true | all-gather | bytes 294912 | tf_op jit(solution)/shard_map/all_gather | solution.py:75
  455.7 0.1 reshape.41
  455.8 0.3 fusion.15
  456.0 10.6 %psum.23 = f32[4,32]{1,0:T(4,128)S(1)} all-reduce(f32[4,32]{1,0:T(4,128)S(1)} %fusion.15), channel_id=1, replica_groups=mesh['dp'=2,'tensor'=4,'fsdp'=4] {'tensor'}, use_global_device_ids=true, to_apply=%region_3.4 | all-reduce | flops 128 | bytes 1024 | tf_op jit(solution)/shard_map/psum | solution.py:82
  466.7 0.6 broadcast_multiply_fusion
  (25 shorter events, 0.1 us)
Async XLA Ops:
  6.5 336.9 %copy-start = (bf16[2752,64]{0,1:T(8,128)(2,1)S(1)}, bf16[2752,64]{0,1:T(8,128)(2,1)}, u32[]{:S(2)}) copy-start(bf16[2752,64]{0,1:T(8,128)(2,1)} %param.18) | copy-start | bytes 1056772
  6.5 212.8 %all-gather.5.cloned.1.call-start = ((), (), s32[]{:S(2)}) async-start(), calls=%async_computation | async-start | bytes 2621440 | tf_op jit(solution)/shard_map/all_gather | solution.py:28
  7.3 215.2 %all-gather.7.cloned.1.call-start = ((), (), s32[]{:S(2)}) async-start(), calls=%async_computation.1 | async-start | bytes 2621440 | tf_op jit(solution)/shard_map/all_gather | solution.py:29
  8.0 316.3 %all-gather.9.cloned.1.call-start = ((), (), s32[]{:S(2)}) async-start(), calls=%async_computation.2 | async-start | bytes 25362432 | tf_op jit(solution)/shard_map/all_gather | solution.py:35
  8.7 435.9 %all-reduce.3.cloned.1.call-start = ((), (), s32[]{:S(2)}) async-start(), calls=%async_computation.3 | async-start | bytes 1048576 | tf_op jit(solution)/shard_map/psum | solution.py:61
  8.8 35.1 %collective-permute-start = (bf16[512,2752]{0,1:T(8,128)(2,1)}, bf16[512,2752]{0,1:T(8,128)(2,1)S(1)}, u32[]{:S(2)}, u32[]{:S(2)}) collective-permute-start(bf16[512,2752]{0,1:T(8,128)(2,1)} %param.17), channel_id=1, source_target_pairs={{0,1},{1,2},{2,3},{3,16},{16,17},{17,18},{18,19},{19,0},{4,5},{5,6... | collective-permute-start | bytes 8454152 | tf_op jit(solution)/shard_map/ppermute | solution.py:45
  43.9 34.2 %collective-permute-start.1 = (bf16[512,2752]{0,1:T(8,128)(2,1)S(1)}, bf16[512,2752]{0,1:T(8,128)(2,1)S(1)}, u32[]{:S(2)}, u32[]{:S(2)}) collective-permute-start(bf16[512,2752]{0,1:T(8,128)(2,1)S(1)} %collective-permute-done), channel_id=1, source_target_pairs={{0,1},{1,2},{2,3},{3,16},{16,17},{17,18},{18,19},{19,0},{4,5},{5,6... | collective-permute-start | bytes 8454152 | tf_op jit(solution)/shard_map/ppermute | solution.py:45
  43.9 64.0 %collective-permute-start.4 = (bf16[512,2752]{0,1:T(8,128)(2,1)}, bf16[512,2752]{0,1:T(8,128)(2,1)}, u32[]{:S(2)}, u32[]{:S(2)}) collective-permute-start(bf16[512,2752]{0,1:T(8,128)(2,1)} %param.17), channel_id=1, source_target_pairs={{0,19},{1,0},{2,1},{3,2},{16,3},{17,16},{18,17},{19,18},{4,23},{5,... | collective-permute-start | bytes 8454152 | tf_op jit(solution)/shard_map/ppermute | solution.py:47
  78.0 1.6 copy-start.2
  79.6 34.3 %collective-permute-start.2 = (bf16[512,2752]{0,1:T(8,128)(2,1)S(1)}, bf16[512,2752]{0,1:T(8,128)(2,1)}, u32[]{:S(2)}, u32[]{:S(2)}) collective-permute-start(bf16[512,2752]{0,1:T(8,128)(2,1)S(1)} %collective-permute-done.1), channel_id=1, source_target_pairs={{0,1},{1,2},{2,3},{3,16},{16,17},{17,18},{18,19},{19,0},{4,5},{5,6... | collective-permute-start | bytes 8454152 | tf_op jit(solution)/shard_map/ppermute | solution.py:45
  107.8 117.8 %collective-permute-start.5 = (bf16[512,2752]{0,1:T(8,128)(2,1)}, bf16[512,2752]{0,1:T(8,128)(2,1)}, u32[]{:S(2)}, u32[]{:S(2)}) collective-permute-start(bf16[512,2752]{0,1:T(8,128)(2,1)} %collective-permute-done.4), channel_id=1, source_target_pairs={{0,19},{1,0},{2,1},{3,2},{16,3},{17,16},{18,17},{19,18},{4,23},{5,... | collective-permute-start | bytes 8454152 | tf_op jit(solution)/shard_map/ppermute | solution.py:47
  113.9 111.7 %collective-permute-start.3 = (bf16[512,2752]{0,1:T(8,128)(2,1)}, bf16[512,2752]{0,1:T(8,128)(2,1)}, u32[]{:S(2)}, u32[]{:S(2)}) collective-permute-start(bf16[512,2752]{0,1:T(8,128)(2,1)} %collective-permute-done.2), channel_id=1, source_target_pairs={{0,1},{1,2},{2,3},{3,16},{16,17},{17,18},{18,19},{19,0},{4,5},{5,6... | collective-permute-start | bytes 8454152 | tf_op jit(solution)/shard_map/ppermute | solution.py:45
  225.6 7.3 %copy-start.3 = (bf16[512,2752]{0,1:T(8,128)(2,1)S(1)}, bf16[512,2752]{0,1:T(8,128)(2,1)}, u32[]{:S(2)}) copy-start(bf16[512,2752]{0,1:T(8,128)(2,1)} %copy-done.2) | copy-start | bytes 8454148
  225.6 75.4 %collective-permute-start.6 = (bf16[512,2752]{0,1:T(8,128)(2,1)}, bf16[512,2752]{0,1:T(8,128)(2,1)S(1)}, u32[]{:S(2)}, u32[]{:S(2)}) collective-permute-start(bf16[512,2752]{0,1:T(8,128)(2,1)} %collective-permute-done.5), channel_id=1, source_target_pairs={{0,19},{1,0},{2,1},{3,2},{16,3},{17,16},{18,17},{19,18},{4,23},{5,... | collective-permute-start | bytes 8454152 | tf_op jit(solution)/shard_map/ppermute | solution.py:47
  232.9 3.6 copy-start.1
  343.4 21.0 %copy-start.4 = (s32[4]{0:T(128)S(1)}, s32[4]{0:T(128)}, u32[]{:S(2)}) copy-start(s32[4]{0:T(128)} %param.15) | copy-start | bytes 52
  343.4 21.0 %copy-start.5 = (s32[4]{0:T(128)S(1)}, s32[4]{0:T(128)}, u32[]{:S(2)}) copy-start(s32[4]{0:T(128)} %param.14) | copy-start | bytes 52
Sparse Core Ops, SparseCore 0:
  8.9 48.3 all-gather.4
  58.9 44.4 all-gather.6
  105.3 206.4 all-gather.8
  364.5 80.0 all-reduce.2
